TPU v7x, 32 devices: a whole 2x2x4 slice. The times are simulated.
32 devices in a mesh: row: 4 (over y, x), col: 8 (over z, core).
Axes of the slice: x: 2, y: 2, z: 4, core: 2. Of those that a mesh axis runs over, the one named last changes fastest.
Arguments:
- inputs: bfloat16 [2048, 25600], P('row', 'col'), may hold values from -6 to 6
- out_grads: bfloat16 [2048, 5120], P('col', 'row'), may hold values from -0.125 to 0.125
- weights: bfloat16 [5120, 25600], P('row', 'col'), may hold values from -3 to 3
- momentum: float32 [5120, 25600], P('row', 'col'), may hold values from -13 to 13
- right_factor: float32 [25600, 256], P('col'), may hold values from -6 to 6
Outputs:
- weights_new: float32 [5120, 25600], P('row', 'col')
- momentum_new: float32 [5120, 25600], P('row', 'col')
- factor_new: float32 [25600, 256], P('col')
All inputs are finite; a program needn't handle non-finite values.
Results may differ from a plain program's by a relative error of at most 0.0003.
Values may be sent and summed in bfloat16 or wider, within the bound.
No kernel may reach another device: no remote copies, remote signals or barrier semaphores. Data moves between devices by JAX's collectives and lax.ppermute only.
A program may use at most 128 MiB of HBM per device.

v0:
```python
import math
import jax
import jax.numpy as jnp
from jax import lax
from jax.sharding import PartitionSpec as P

M = 5120
N = 25600
RANK = 256
mix_rate = 0.95
step_rate = 0.3
weight_decay = 0.1
tiny_eps = 1e-06
highest = lax.Precision.HIGHEST


def inner_rows(left_side, right_in):
    return lax.dot_general(left_side, right_in, (((0,), (0,)), ((), ())), precision=highest)


def orthonormal(sketch_rows, gram_total):
    factor_low = jnp.linalg.cholesky(gram_total)
    return jax.scipy.linalg.solve_triangular(factor_low, sketch_rows.T, lower=True).T


def on_device(inputs, out_grads, weights, momentum, right_factor):
    grads_all = lax.all_gather(out_grads, "col", axis=0, tiled=True)
    gradient = lax.dot_general(
        grads_all,
        lax.all_gather(inputs, "row", axis=0, tiled=True),
        (((0,), (0,)), ((), ())),
        preferred_element_type=jnp.float32,
    )
    moment = momentum + gradient
    sketch_part = jnp.dot(moment, right_factor, precision=highest)
    sketch_rows = lax.psum(sketch_part, "col")
    gram_total = lax.psum(inner_rows(sketch_rows, sketch_rows), "row")
    basis_rows = orthonormal(sketch_rows, gram_total)
    right_part = inner_rows(moment, basis_rows)
    right_share = lax.psum_scatter(right_part, "row", scatter_dimension=0, tiled=True)
    squares = lax.psum(jnp.sum(right_share * right_share, axis=0), ("row", "col"))
    right_side = lax.all_gather(right_share, "row", axis=0, tiled=True)
    column_scale = lax.rsqrt(squares / N + tiny_eps)
    factor_new = right_side * column_scale
    momentum_new = moment - (1.0 - mix_rate) * jnp.dot(basis_rows, right_side.T, precision=highest)
    update = jnp.dot(basis_rows, factor_new.T, precision=highest)
    weights_new = (
        weights.astype(jnp.float32) * (1.0 - step_rate * weight_decay)
        - step_rate * math.sqrt(M / RANK) * update
    )
    return (weights_new, momentum_new, factor_new)


def solution(mesh):
    placed = (P("row", "col"), P("col", "row"), P("row", "col"), P("row", "col"), P("col", None))
    return jax.shard_map(
        on_device,
        mesh=mesh,
        in_specs=placed,
        out_specs=(P("row", "col"), P("row", "col"), P("col", None)),
        check_vma=False,
    )
```

profile of v0, /device:TPU:0, one launch (start us, length us, event | category | flops | bytes accessed | tf_op | source)
XLA Modules:
  0.0 616.2 jit_solution(3706774686516627048)
XLA Ops:
  8.7 59.7 %all-gather.4.cloned.1.call-done = bf16[2048,1280]{1,0:T(8,128)(2,1)} async-done(((bf16[256,1280]{1,0:T(8,128)(2,1)}), bf16[2048,1280]{1,0:T(8,128)(2,1)}) %all-gather.4.cloned.1.call-update) | async-done | bytes 5242896 | tf_op jit(solution)/shard_map/all_gather | solution.py:27
  68.4 127.4 %all-gather.6.cloned.1.call-done = bf16[2048,3200]{1,0:T(8,128)(2,1)} async-done(((bf16[512,3200]{1,0:T(8,128)(2,1)}), bf16[2048,3200]{1,0:T(8,128)(2,1)}) %all-gather.6.cloned.1.call-update) | async-done | bytes 13107216 | tf_op jit(solution)/shard_map/all_gather | solution.py:30
  195.8 29.4 %convolution_add_fusion = f32[1280,3200]{1,0:T(8,128)} fusion(f32[1280,3200]{1,0:T(8,128)} %param.8, bf16[2048,1280]{1,0:T(8,128)(2,1)} %all-gather.4.cloned.1.call-done, bf16[2048,3200]{1,0:T(8,128)(2,1)} %all-gather.6.cloned.1.call-done), kind=kOutput, calls=%fused_computation.2 | convolution fusion | flops 16781312000 | bytes 51118080 | tf_op jit(solution)/shard_map/dot_general | solution.py:28
  225.1 17.8 %fusion.15 = f32[1280,256]{1,0:T(8,128)} fusion(f32[1280,3200]{1,0:T(8,128)} %convolution_add_fusion, f32[3200,256]{1,0:T(8,128)S(1)} %copy-done), kind=kOutput, calls=%fused_computation.41 | convolution fusion | flops 12582912000 | bytes 20971520 | tf_op jit(solution)/shard_map/dot_general | solution.py:35
  243.0 60.5 %all-reduce.4.cloned.1.call-done = f32[1280,256]{1,0:T(8,128)} async-done(((f32[1280,256]{1,0:T(8,128)}), f32[1280,256]{1,0:T(8,128)}) %all-reduce.4.cloned.1.call-update) | async-done | bytes 1310736 | tf_op jit(solution)/shard_map/psum | solution.py:36
  303.5 4.8 fusion.16
  308.6 42.0 %all-reduce.6.cloned.1.call-done = f32[256,256]{0,1:T(8,128)} async-done(((f32[256,256]{0,1:T(8,128)}), f32[256,256]{0,1:T(8,128)}) %all-reduce.6.cloned.1.call-update) | async-done | bytes 262160 | tf_op jit(solution)/shard_map/psum | solution.py:37
  350.6 1.1 copy.9
  352.7 11.7 %cholesky.50 = f32[128,128]{1,0:T(8,128)S(1)} custom-call(f32[128,128]{1,0:T(8,128)S(1)} %cholesky.118), custom_call_target="Cholesky" | custom-call | tf_op jit(solution)/shard_map/jit(cholesky)/cholesky | solution.py:22
  364.4 9.8 %custom-call.15 = f32[1,128,128]{1,2,0:T(8,128)S(1)} custom-call(f32[1,128,128]{2,1,0:T(8,128)S(1)} %get-tuple-element.24), custom_call_target="InvertDiagBlocksLowerTriangular" | custom-call | tf_op jit(solution)/shard_map/jit(cholesky)/cholesky | solution.py:22
  374.8 11.7 %cholesky.105 = f32[128,128]{1,0:T(8,128)S(1)} custom-call(f32[128,128]{1,0:T(8,128)S(1)} %convolution_subtract_fusion.1), custom_call_target="Cholesky" | custom-call | tf_op jit(solution)/shard_map/jit(cholesky)/cholesky | solution.py:22
  388.6 4.2 while.1
  389.4 1.4 bitcast_dynamic-update-slice_fusion.2
  391.4 1.4 bitcast_dynamic-update-slice_fusion.2
  392.8 19.7 %custom-call.16 = f32[2,128,128]{1,2,0:T(8,128)S(1)} custom-call(f32[2,128,128]{2,1,0:T(8,128)S(1)} %get-tuple-element.10), custom_call_target="InvertDiagBlocksLowerTriangular" | custom-call | tf_op jit(solution)/shard_map/jit(_solve_triangular)/triangular_solve | solution.py:23
  413.3 1.2 convolution_subtract_fusion
  415.2 32.1 %fusion.2 = f32[3200,256]{1,0:T(8,128)} fusion(f32[1280,3200]{1,0:T(8,128)} %convolution_add_fusion, f32[128,1280]{1,0:T(8,128)S(1)} %fusion.7, f32[128,1280]{1,0:T(8,128)S(1)} %fusion.3), kind=kOutput, calls=%fused_computation.11 | convolution fusion | flops 12583239680 | bytes 20971520 | tf_op jit(solution)/shard_map/dot_general | solution.py:18
  447.4 45.1 %reduce-scatter.2.cloned.1.call-done = f32[800,256]{1,0:T(8,128)} async-done(((f32[3200,256]{1,0:T(8,128)}), f32[800,256]{1,0:T(8,128)}) %reduce-scatter.2.cloned.1.call-update) | async-done | bytes 819216 | tf_op jit(solution)/shard_map/reduce_scatter | solution.py:40
  492.6 1.3 multiply_reduce_fusion
  493.8 40.3 %psum.23 = f32[256]{0:T(256)S(1)} all-reduce(f32[256]{0:T(256)S(1)} %multiply_reduce_fusion), channel_id=1, replica_groups=mesh['row'=4,'col'=8] {'row','col'}, use_global_device_ids=true, to_apply=%region_8.9 | all-reduce | flops 256 | bytes 2048 | tf_op jit(solution)/shard_map/psum | solution.py:41
  534.1 6.0 all-gather.8.cloned.1.call-done
  540.1 2.1 broadcast_multiply_fusion
  542.3 32.8 %fusion.1 = f32[1280,3200]{1,0:T(8,128)} fusion(f32[3200,256]{1,0:T(8,128)S(1)} %broadcast_multiply_fusion, bf16[1280,3200]{1,0:T(8,128)(2,1)} %param.7, f32[128,1280]{1,0:T(8,128)S(1)} %fusion.7, f32[128,1280]{1,0:T(8,128)S(1)} %fusion.3), kind=kOutput, calls=%fused_computation.6 | convolution fusion | flops 12599623680 | bytes 29163520 | tf_op jit(solution)/shard_map/dot_general | solution.py:46
  575.0 34.1 %fusion = f32[1280,3200]{1,0:T(8,128)} fusion(f32[1280,3200]{1,0:T(8,128)} %convolution_add_fusion, f32[3200,256]{1,0:T(8,128)S(1)} %copy-done.4, f32[128,1280]{1,0:T(8,128)} %copy-done.6, f32[128,1280]{1,0:T(8,128)} %copy-done.2), kind=kOutput, calls=%fused_computation.4 | convolution fusion | flops 12591431680 | bytes 37355520 | tf_op jit(solution)/shard_map/dot_general | solution.py:45
  (45 shorter events, 7.0 us)
Async XLA Ops:
  7.2 217.9 %copy-start = (f32[3200,256]{1,0:T(8,128)S(1)}, f32[3200,256]{1,0:T(8,128)}, u32[]{:S(2)}) copy-start(f32[3200,256]{1,0:T(8,128)} %param.9) | copy-start | bytes 9830404
  7.2 61.2 %all-gather.4.cloned.1.call-start = ((), (), s32[]{:S(2)}) async-start(), calls=%async_computation.1 | async-start | bytes 5898240 | tf_op jit(solution)/shard_map/all_gather | solution.py:27
  7.9 187.8 %all-gather.6.cloned.1.call-start = ((), (), s32[]{:S(2)}) async-start(), calls=%async_computation.2 | async-start | bytes 16384000 | tf_op jit(solution)/shard_map/all_gather | solution.py:30
  8.7 294.8 %all-reduce.4.cloned.1.call-start = ((), (), s32[]{:S(2)}) async-start(), calls=%async_computation.3 | async-start | bytes 2621440 | tf_op jit(solution)/shard_map/psum | solution.py:36
  242.9 107.7 %all-reduce.6.cloned.1.call-start = ((), (), s32[]{:S(2)}) async-start(), calls=%async_computation.4 | async-start | bytes 524288 | tf_op jit(solution)/shard_map/psum | solution.py:37
  303.5 109.0 %copy-start.5 = (f32[1280,256]{1,0:T(8,128)S(1)}, f32[1280,256]{1,0:T(8,128)}, u32[]{:S(2)}) copy-start(f32[1280,256]{1,0:T(8,128)} %all-reduce.4.cloned.1.call-done) | copy-start | bytes 3932164
  308.4 184.2 %reduce-scatter.2.cloned.1.call-start = ((), (), s32[]{:S(2)}) async-start(), calls=%async_computation.5 | async-start | bytes 4096000 | tf_op jit(solution)/shard_map/reduce_scatter | solution.py:40
  413.3 129.0 %copy-start.2 = (f32[128,1280]{1,0:T(8,128)}, f32[128,1280]{1,0:T(8,128)S(1)}, u32[]{:S(2)}) copy-start(f32[128,1280]{1,0:T(8,128)S(1)} %fusion.3) | copy-start | bytes 1966084
  415.2 127.0 %copy-start.6 = (f32[128,1280]{1,0:T(8,128)}, f32[128,1280]{1,0:T(8,128)S(1)}, u32[]{:S(2)}) copy-start(f32[128,1280]{1,0:T(8,128)S(1)} %fusion.7) | copy-start | bytes 1966084
  447.4 92.7 %all-gather.8.cloned.1.call-start = ((), (), s32[]{:S(2)}) async-start(), calls=%async_computation.6 | async-start | bytes 4096000 | tf_op jit(solution)/shard_map/all_gather | solution.py:42
  542.2 32.8 %copy-start.3 = (f32[3200,256]{1,0:T(8,128)}, f32[3200,256]{1,0:T(8,128)S(1)}, u32[]{:S(2)}) copy-start(f32[3200,256]{1,0:T(8,128)S(1)} %broadcast_multiply_fusion) | copy-start | bytes 9830404
  542.3 32.8 %copy-start.4 = (f32[3200,256]{1,0:T(8,128)S(1)}, f32[3200,256]{1,0:T(8,128)}, u32[]{:S(2)}) copy-start(f32[3200,256]{1,0:T(8,128)} %all-gather.8.cloned.1.call-done) | copy-start | bytes 9830404
  575.0 34.1 %copy-start.1 = (f32[3200,256]{1,0:T(8,128)S(1)}, f32[3200,256]{1,0:T(8,128)}, u32[]{:S(2)}) copy-start(f32[3200,256]{1,0:T(8,128)} %param.9) | copy-start | bytes 9830404
Sparse Core Ops, SparseCore 0:
  9.6 58.6 all-gather.3
  70.2 125.5 all-gather.5
  243.0 60.4 all-reduce.3
  308.5 42.0 all-reduce.5
  447.5 44.9 reduce-scatter.1
  494.2 45.7 all-gather.7
where the time goes:
time: 623 us; the launch traced here: 616 us
  waiting for transfers between devices  342 us (55%)
  matrix products  154 us (25%)
  other arithmetic  58.1 us (9%)
  blocking collectives  40.3 us (6%)
  between operations  15.8 us (3%)
    all_gather x1, waiting for transfers between devices, on_device(): lax.all_gather(inputs, 'row', axis=0, tiled=True)  127 us
    psum x1, waiting for transfers between devices, on_device(): sketch_rows = lax.psum(sketch_part, 'col')  60.5 us
    all_gather x1, waiting for transfers between devices, on_device(): grads_all = lax.all_gather(out_grads, 'col', axis=0, tiled=True)  59.7 us
    reduce_scatter x1, waiting for transfers between devices, on_device(): lax.psum_scatter(right_part, 'row', scatter_dimension=0, tiled=True)  45.1 us
    psum x1, waiting for transfers between devices, on_device(): gram_total = lax.psum(inner_rows(sketch_rows, sketch_rows), 'row')  42 us
    psum x1, blocking collectives, on_device(): lax.psum(jnp.sum(right_share * right_share, axis=0), ('row', 'col'))  40.3 us
    dot_general x2, matrix products, inner_rows(): lax.dot_general(left_side, right_in, (((0,), (0,)), ((), ())), precision=...  36.9 us
    dot_general x1, matrix products, on_device(): jnp.dot(basis_rows, right_side.T, precision=highest)  34.1 us
  transfers between devices with their start and end apart: 6, of which 6 were waited for; matrix products, arithmetic and copies ran while one was open for 0% of the time, Pallas kernels for 0%

commit v1 on v0

--- a/solution.py
+++ b/solution.py
@@ -33,7 +33,13 @@
     )
     moment = momentum + gradient
     sketch_part = jnp.dot(moment, right_factor, precision=highest)
-    sketch_rows = lax.psum(sketch_part, "col")
+    peers = lax.axis_size("col")
+    sketch_rows, stride = (sketch_part, 1)
+    while stride < peers:
+        sketch_rows = sketch_rows + lax.ppermute(
+            sketch_rows, "col", [(i, i ^ stride) for i in range(peers)]
+        )
+        stride = 2 * stride
     gram_total = lax.psum(inner_rows(sketch_rows, sketch_rows), "row")
     basis_rows = orthonormal(sketch_rows, gram_total)
     right_part = inner_rows(moment, basis_rows)

time: 623 us -> 653 us (1.048)
  waiting for transfers between devices: 342 us -> 370 us
    ppermute x0 -> x3, waiting for transfers between devices: none -> 88.9 us  [on_device(): lax.ppermute(sketch_rows, 'col', [(i, i ^ stride) for i in range(peers)])]
    psum x1 -> x0, waiting for transfers between devices: 60.5 us -> none  [on_device(): sketch_rows = lax.psum(sketch_part, 'col')]
  transfers between devices with their start and end apart: 6 -> 8, of which waited for: 6 -> 8; matrix products, arithmetic and copies ran while one was open for 0% -> 0% of each run, Pallas kernels for 0% -> 0%
where the time goes in v1:
time: 653 us; the launch traced here: 646 us
  waiting for transfers between devices  370 us (57%)
  matrix products  151 us (23%)
  other arithmetic  59.9 us (9%)
  blocking collectives  40.2 us (6%)
  between operations  15.7 us (2%)
    all_gather x1, waiting for transfers between devices, on_device(): lax.all_gather(inputs, 'row', axis=0, tiled=True)  127 us
    ppermute x3, waiting for transfers between devices, on_device(): lax.ppermute(sketch_rows, 'col', [(i, i ^ stride) for i in range(peers)])  88.9 us
    all_gather x1, waiting for transfers between devices, on_device(): grads_all = lax.all_gather(out_grads, 'col', axis=0, tiled=True)  59.7 us
    reduce_scatter x1, waiting for transfers between devices, on_device(): lax.psum_scatter(right_part, 'row', scatter_dimension=0, tiled=True)  45.1 us
    psum x1, waiting for transfers between devices, on_device(): gram_total = lax.psum(inner_rows(sketch_rows, sketch_rows), 'row')  41.2 us
    psum x1, blocking collectives, on_device(): lax.psum(jnp.sum(right_share * right_share, axis=0), ('row', 'col'))  40.2 us
    dot_general x2, matrix products, inner_rows(): lax.dot_general(left_side, right_in, (((0,), (0,)), ((), ())), precision=...  34.8 us
    another operation x6, other arithmetic, orthonormal(): factor_low = jnp.linalg.cholesky(gram_total)  34 us
  transfers between devices with their start and end apart: 8, of which 8 were waited for; matrix products, arithmetic and copies ran while one was open for 0% of the time, Pallas kernels for 0%

profile of v1, /device:TPU:0, one launch (start us, length us, event | category | flops | bytes accessed | tf_op | source)
XLA Modules:
  0.0 646.2 jit_solution(17672954261898459536)
XLA Ops:
  8.7 59.7 %all-gather.4.cloned.1.call-done = bf16[2048,1280]{1,0:T(8,128)(2,1)} async-done(((bf16[256,1280]{1,0:T(8,128)(2,1)}), bf16[2048,1280]{1,0:T(8,128)(2,1)}) %all-gather.4.cloned.1.call-update) | async-done | bytes 5242896 | tf_op jit(solution)/shard_map/all_gather | solution.py:27
  68.4 127.4 %all-gather.6.cloned.1.call-done = bf16[2048,3200]{1,0:T(8,128)(2,1)} async-done(((bf16[512,3200]{1,0:T(8,128)(2,1)}), bf16[2048,3200]{1,0:T(8,128)(2,1)}) %all-gather.6.cloned.1.call-update) | async-done | bytes 13107216 | tf_op jit(solution)/shard_map/all_gather | solution.py:30
  195.8 29.4 %convolution_add_fusion = f32[1280,3200]{1,0:T(8,128)} fusion(f32[1280,3200]{1,0:T(8,128)} %param.8, bf16[2048,1280]{1,0:T(8,128)(2,1)} %all-gather.4.cloned.1.call-done, bf16[2048,3200]{1,0:T(8,128)(2,1)} %all-gather.6.cloned.1.call-done), kind=kOutput, calls=%fused_computation.2 | convolution fusion | flops 16781312000 | bytes 51118080 | tf_op jit(solution)/shard_map/dot_general | solution.py:28
  225.1 16.8 %fusion.18 = f32[1280,256]{1,0:T(8,128)S(1)} fusion(f32[1280,3200]{1,0:T(8,128)} %convolution_add_fusion, f32[3200,256]{1,0:T(8,128)S(1)} %copy-done), kind=kOutput, calls=%fused_computation.45 | convolution fusion | flops 12582912000 | bytes 20971520 | tf_op jit(solution)/shard_map/dot_general | solution.py:35
  242.0 3.0 collective-permute-done
  245.2 1.6 collective-permute-start.1
  246.8 29.3 %collective-permute-done.1 = f32[1280,256]{1,0:T(8,128)S(1)} collective-permute-done((f32[1280,256]{1,0:T(8,128)S(1)}, f32[1280,256]{1,0:T(8,128)S(1)}, u32[]{:S(2)}, u32[]{:S(2)}) %collective-permute-start.1) | collective-permute-done | bytes 1310752 | tf_op jit(solution)/shard_map/ppermute | solution.py:39
  276.3 2.5 collective-permute-start.2
  278.7 56.5 %collective-permute-done.2 = f32[1280,256]{1,0:T(8,128)S(1)} collective-permute-done((f32[1280,256]{1,0:T(8,128)S(1)}, f32[1280,256]{1,0:T(8,128)S(1)}, u32[]{:S(2)}, u32[]{:S(2)}) %collective-permute-start.2) | collective-permute-done | bytes 1310752 | tf_op jit(solution)/shard_map/ppermute | solution.py:39
  335.3 3.0 fusion.6
  338.8 1.5 add_bitcast_fusion
  340.2 41.2 %all-reduce.3.cloned.1.call-done = f32[256,256]{0,1:T(8,128)} async-done(((f32[256,256]{0,1:T(8,128)}), f32[256,256]{0,1:T(8,128)}) %all-reduce.3.cloned.1.call-update) | async-done | bytes 262160 | tf_op jit(solution)/shard_map/psum | solution.py:43
  383.6 11.7 %cholesky.50 = f32[128,128]{1,0:T(8,128)S(1)} custom-call(f32[128,128]{1,0:T(8,128)S(1)} %cholesky.118), custom_call_target="Cholesky" | custom-call | tf_op jit(solution)/shard_map/jit(cholesky)/cholesky | solution.py:22
  395.3 9.8 %custom-call.15 = f32[1,128,128]{1,2,0:T(8,128)S(1)} custom-call(f32[1,128,128]{2,1,0:T(8,128)S(1)} %get-tuple-element.24), custom_call_target="InvertDiagBlocksLowerTriangular" | custom-call | tf_op jit(solution)/shard_map/jit(cholesky)/cholesky | solution.py:22
  405.6 11.7 %cholesky.105 = f32[128,128]{1,0:T(8,128)S(1)} custom-call(f32[128,128]{1,0:T(8,128)S(1)} %convolution_subtract_fusion), custom_call_target="Cholesky" | custom-call | tf_op jit(solution)/shard_map/jit(cholesky)/cholesky | solution.py:22
  419.4 4.0 while.1
  423.4 19.7 %custom-call.16 = f32[2,128,128]{1,2,0:T(8,128)S(1)} custom-call(f32[2,128,128]{2,1,0:T(8,128)S(1)} %get-tuple-element.10), custom_call_target="InvertDiagBlocksLowerTriangular" | custom-call | tf_op jit(solution)/shard_map/jit(_solve_triangular)/triangular_solve | solution.py:23
  445.8 31.8 %fusion.2 = f32[3200,256]{1,0:T(8,128)} fusion(f32[1280,3200]{1,0:T(8,128)} %convolution_add_fusion, f32[128,1280]{1,0:T(8,128)S(1)} %fusion.3, f32[128,1280]{1,0:T(8,128)S(1)} %fusion.4), kind=kOutput, calls=%fused_computation.10 | convolution fusion | flops 12583239680 | bytes 20971520 | tf_op jit(solution)/shard_map/dot_general | solution.py:18
  477.8 45.1 %reduce-scatter.2.cloned.1.call-done = f32[800,256]{1,0:T(8,128)} async-done(((f32[3200,256]{1,0:T(8,128)}), f32[800,256]{1,0:T(8,128)}) %reduce-scatter.2.cloned.1.call-update) | async-done | bytes 819216 | tf_op jit(solution)/shard_map/reduce_scatter | solution.py:46
  524.2 40.2 %psum.15 = f32[256]{0:T(256)S(1)} all-reduce(f32[256]{0:T(256)S(1)} %multiply_reduce_fusion), channel_id=1, replica_groups=mesh['row'=4,'col'=8] {'row','col'}, use_global_device_ids=true, to_apply=%region_7.8 | all-reduce | flops 256 | bytes 2048 | tf_op jit(solution)/shard_map/psum | solution.py:47
  564.4 6.0 all-gather.8.cloned.1.call-done
  570.4 2.1 broadcast_multiply_fusion
  572.6 32.8 %fusion.1 = f32[1280,3200]{1,0:T(8,128)} fusion(f32[3200,256]{1,0:T(8,128)S(1)} %broadcast_multiply_fusion, bf16[1280,3200]{1,0:T(8,128)(2,1)} %param.7, f32[128,1280]{1,0:T(8,128)S(1)} %fusion.3, f32[128,1280]{1,0:T(8,128)S(1)} %fusion.4), kind=kOutput, calls=%fused_computation.6 | convolution fusion | flops 12599623680 | bytes 29163520 | tf_op jit(solution)/shard_map/dot_general | solution.py:52
  605.4 33.9 %fusion = f32[1280,3200]{1,0:T(8,128)} fusion(f32[1280,3200]{1,0:T(8,128)} %convolution_add_fusion, f32[3200,256]{1,0:T(8,128)S(1)} %copy-done.4, f32[128,1280]{1,0:T(8,128)} %copy-done.5, f32[128,1280]{1,0:T(8,128)} %copy-done.2), kind=kOutput, calls=%fused_computation.4 | convolution fusion | flops 12591431680 | bytes 37355520 | tf_op jit(solution)/shard_map/dot_general | solution.py:51
  (51 shorter events, 13.8 us)
Async XLA Ops:
  7.2 217.9 %copy-start = (f32[3200,256]{1,0:T(8,128)S(1)}, f32[3200,256]{1,0:T(8,128)}, u32[]{:S(2)}) copy-start(f32[3200,256]{1,0:T(8,128)} %param.9) | copy-start | bytes 9830404
  7.2 61.2 %all-gather.4.cloned.1.call-start = ((), (), s32[]{:S(2)}) async-start(), calls=%async_computation.1 | async-start | bytes 5898240 | tf_op jit(solution)/shard_map/all_gather | solution.py:27
  7.9 187.8 %all-gather.6.cloned.1.call-start = ((), (), s32[]{:S(2)}) async-start(), calls=%async_computation.2 | async-start | bytes 16384000 | tf_op jit(solution)/shard_map/all_gather | solution.py:30
  8.7 372.8 %all-reduce.3.cloned.1.call-start = ((), (), s32[]{:S(2)}) async-start(), calls=%async_computation.3 | async-start | bytes 524288 | tf_op jit(solution)/shard_map/psum | solution.py:43
  241.9 3.1 collective-permute-start
  245.2 30.9 %collective-permute-start.1 = (f32[1280,256]{1,0:T(8,128)S(1)}, f32[1280,256]{1,0:T(8,128)S(1)}, u32[]{:S(2)}, u32[]{:S(2)}) collective-permute-start(f32[1280,256]{1,0:T(8,128)S(1)} %add.48), channel_id=1, source_target_pairs={{0,2},{1,3},{2,0},{3,1},{4,6},{5,7},{6,4},{7,5},{8,10},{9,11},{10,... | collective-permute-start | bytes 3932168 | tf_op jit(solution)/shard_map/ppermute | solution.py:39
  276.3 59.0 %collective-permute-start.2 = (f32[1280,256]{1,0:T(8,128)S(1)}, f32[1280,256]{1,0:T(8,128)S(1)}, u32[]{:S(2)}, u32[]{:S(2)}) collective-permute-start(f32[1280,256]{1,0:T(8,128)S(1)} %add.49), channel_id=1, source_target_pairs={{0,4},{1,5},{2,6},{3,7},{4,0},{5,1},{6,2},{7,3},{8,12},{9,13},{10,... | collective-permute-start | bytes 3932168 | tf_op jit(solution)/shard_map/ppermute | solution.py:39
  335.3 3.0 copy-start.6
  338.3 184.6 %reduce-scatter.2.cloned.1.call-start = ((), (), s32[]{:S(2)}) async-start(), calls=%async_computation.4 | async-start | bytes 4096000 | tf_op jit(solution)/shard_map/reduce_scatter | solution.py:46
  443.9 128.7 %copy-start.2 = (f32[128,1280]{1,0:T(8,128)}, f32[128,1280]{1,0:T(8,128)S(1)}, u32[]{:S(2)}) copy-start(f32[128,1280]{1,0:T(8,128)S(1)} %fusion.4) | copy-start | bytes 1966084
  445.8 126.7 %copy-start.5 = (f32[128,1280]{1,0:T(8,128)}, f32[128,1280]{1,0:T(8,128)S(1)}, u32[]{:S(2)}) copy-start(f32[128,1280]{1,0:T(8,128)S(1)} %fusion.3) | copy-start | bytes 1966084
  477.7 92.7 %all-gather.8.cloned.1.call-start = ((), (), s32[]{:S(2)}) async-start(), calls=%async_computation.5 | async-start | bytes 4096000 | tf_op jit(solution)/shard_map/all_gather | solution.py:48
  572.6 32.8 %copy-start.3 = (f32[3200,256]{1,0:T(8,128)}, f32[3200,256]{1,0:T(8,128)S(1)}, u32[]{:S(2)}) copy-start(f32[3200,256]{1,0:T(8,128)S(1)} %broadcast_multiply_fusion) | copy-start | bytes 9830404
  572.6 32.8 %copy-start.4 = (f32[3200,256]{1,0:T(8,128)S(1)}, f32[3200,256]{1,0:T(8,128)}, u32[]{:S(2)}) copy-start(f32[3200,256]{1,0:T(8,128)} %all-gather.8.cloned.1.call-done) | copy-start | bytes 9830404
  605.3 33.9 %copy-start.1 = (f32[3200,256]{1,0:T(8,128)S(1)}, f32[3200,256]{1,0:T(8,128)}, u32[]{:S(2)}) copy-start(f32[3200,256]{1,0:T(8,128)} %param.9) | copy-start | bytes 9830404
Sparse Core Ops, SparseCore 0:
  9.6 58.6 all-gather.3
  70.2 125.5 all-gather.5
  338.4 43.0 all-reduce.2
  477.8 44.9 reduce-scatter.1
  524.6 45.7 all-gather.7
